TPU v7x, 32 devices: a whole 2x2x4 slice. The times are simulated.
32 devices in a mesh: subj: 2 (over x), row: 8 (over z, y), col: 2 (over core).
Axes of the slice: x: 2, y: 2, z: 4, core: 2. Of those that a mesh axis runs over, the one named last changes fastest.
Arguments:
- series: float32 [256, 11392], P(('subj', 'row', 'col')), parts along dimension 0, may hold values from -30 to 30
- tap_values: float32 [17], replicated, may hold values from -4 to 4
- tap_count: int32 [1], replicated, may hold values from 4 to 8
- kept_frames: int32 [32], P('subj'), parts along dimension 0, may hold values from 1 to 8, 96 in all
- band_start: int32 [2], P('subj'), parts along dimension 0, may hold values from 0 to 7296
Outputs:
- fisher_band: bfloat16 [8192, 11392], P('subj', ('row', 'col')), parts along dimension 0
There are 2 independent parts, one for each index of `subj`. A program takes and returns all parts, laid end to end along the dimension named above; an argument that names none is the same for every part. Nothing has to cross between parts.
Inputs may be any that keep to these rules, and one draw needn't show every extreme that they name: `tap_count`: frames farther than this from the centre get no weight. Time block d holds frames d * 8 to (d + 1) * 8 - 1; only its first kept_frames[d] frames are kept. `band_start`: the 4096 band grayordinates lie inside the grid.
All inputs are finite; a program needn't handle non-finite values.
Results may differ from a plain program's by a relative error of at most 0.0031.
The roundings to bfloat16 on the way count: a program that leaves them out, or rounds other values in their place, can miss the bound.
Values may be sent and summed in bfloat16 or wider, within the bound.
No kernel may reach another device: no remote copies, remote signals or barrier semaphores. Data moves between devices by JAX's collectives and lax.ppermute only.
A program may use at most 128 MiB of HBM per device.

v0:
```python
import jax
import jax.numpy as jnp
from jax import lax
from jax.sharding import PartitionSpec as P

B = 4096
EPSILON = 1e-06
CLIP_LIMIT = 0.999


def with_halo(cells, sides, width):
    for axis, dim in sides:
        count = lax.axis_size(axis)
        ends = count - 1
        head = lax.slice_in_dim(cells, 0, width, axis=dim)
        tail = lax.slice_in_dim(cells, cells.shape[dim] - width, cells.shape[dim], axis=dim)
        cells = jnp.concatenate(
            [
                lax.ppermute(tail, axis, [(i, (i + 1) % count) for i in range(ends)]),
                cells,
                lax.ppermute(head, axis, [((i + 1) % count, i) for i in range(ends)]),
            ],
            axis=dim,
        )
    return cells


def tap_table(tap_values, tap_count):
    tap_reach = tap_values.shape[0] // 2
    offsets = jnp.arange(tap_values.shape[0], dtype=jnp.int32) - tap_reach
    active = (jnp.abs(offsets) <= tap_count[0]).astype(jnp.float32)
    centre = jnp.sum(active * tap_values) / jnp.sum(active)
    return active * (tap_values - centre)


def band_filter(padded, tap_weights, length):
    filtered = tap_weights[0] * padded[0:length]
    for tap_index in range(1, tap_weights.shape[0]):
        filtered = filtered + tap_weights[tap_index] * padded[tap_index : tap_index + length]
    return filtered


def fisher_z(correlation):
    clipped = jnp.clip(correlation, -CLIP_LIMIT, CLIP_LIMIT)
    return 0.5 * (jnp.log1p(clipped) - jnp.log1p(-clipped))


def body(series, tap_values, tap_count, kept_frames, band_start):
    tap_reach = tap_values.shape[0] // 2
    tap_weights = tap_table(tap_values, tap_count)
    block_len = series.shape[0]
    padded = with_halo(series, ((("row", "col"), 0),), tap_reach)
    filtered = band_filter(padded, tap_weights, block_len)
    own_kept = kept_frames[lax.axis_index(("row", "col"))]
    keep_mask = (jnp.arange(block_len, dtype=jnp.int32) < own_kept).astype(jnp.float32)[:, None]
    centered = keep_mask * filtered
    spread = lax.psum(jnp.sum(centered * centered, axis=0), ("row", "col"))
    scaled = (centered * lax.rsqrt(spread + EPSILON)).astype(jnp.bfloat16)
    columns = lax.all_to_all(scaled, ("row", "col"), split_axis=1, concat_axis=0, tiled=True)
    band_slice = lax.dynamic_slice_in_dim(scaled, band_start[0], B, 1)
    band_cols = lax.all_gather(band_slice, ("row", "col"), axis=0, tiled=True)
    correlation = lax.dot_general(
        band_cols, columns, (((0,), (0,)), ((), ())), preferred_element_type=jnp.float32
    )
    return fisher_z(correlation).astype(jnp.bfloat16)


def solution(mesh):
    placed = (P(("subj", "row", "col"), None), P(), P(), P("subj"), P("subj"))
    return jax.shard_map(
        body, mesh=mesh, in_specs=placed, out_specs=P("subj", ("row", "col")), check_vma=False
    )
```

profile of v0, /device:TPU:0, one launch (start us, length us, event | category | flops | bytes accessed | tf_op | source)
XLA Modules:
  0.0 151.6 jit_solution(5790544908060387476)
XLA Ops:
  6.5 0.0 all-gather.2.cloned.1.call-start
  6.5 2.4 %collective-permute-start = (f32[8,11392]{1,0:T(8,128)}, f32[8,11392]{1,0:T(8,128)S(1)}, u32[]{:S(2)}, u32[]{:S(2)}) collective-permute-start(f32[8,11392]{1,0:T(8,128)} %param.5), channel_id=1, source_target_pairs={{0,1},{1,2},{2,3},{3,4},{4,5},{5,6},{6,7},{7,8},{8,9},{9,10},{10,1... | collective-permute-start | bytes 1093640 | tf_op jit(solution)/shard_map/ppermute | solution.py:19
  8.9 1.3 collective-permute-start.1
  10.9 1.3 dynamic_slice.6
  12.1 1.3 convert_reduce_fusion
  13.5 0.6 compare_convert_fusion
  16.1 0.7 subtract_select_fusion
  16.7 0.7 fusion.19
  17.4 0.0 collective-permute-done
  17.5 1.0 constant_dynamic-update-slice_fusion
  18.5 0.0 collective-permute-done.1
  18.6 12.4 %multiply_reduce_fusion = (f32[11392]{0:T(1024)S(1)}, f32[8,11392]{1,0:T(8,128)S(1)}) fusion(f32[8,11392]{1,0:T(8,128)S(1)} %collective-permute-done.1, f32[]{:T(128)} %bitcast.18, f32[16,11392]{1,0:T(8,128)S(1)} %constant_dynamic-update-slice_fusion.2, f32[]{:T(128)} %bitcast.17, f32[]{:T(128)} %bitcast.16, f32[]{:T(128)} %bitcast.15, f32[]{:T(128)} %bitcast.14, ...), kind=kLoop, calls=%fused_computation.33 | loop fusion | flops 3269504 | bytes 6607460 | tf_op jit(solution)/shard_map/reduce_sum | solution.py:57
  31.0 63.9 %psum.7 = f32[11392]{0:T(1024)S(1)} all-reduce(f32[11392]{0:T(1024)S(1)} %get-tuple-element.5), channel_id=1, replica_groups=mesh['subj'=2,'row'=8,'col'=2] {'row','col'}, use_global_device_ids=true, to_apply=%region_3.0 | all-reduce | flops 11392 | bytes 91136 | tf_op jit(solution)/shard_map/psum | solution.py:57
  94.9 0.7 constant_dynamic-slice_fusion
  95.7 0.0 all-gather.2.cloned.1.call-update
  95.7 0.4 all_to_all.14
  96.1 0.1 copy.6
  96.2 12.3 %all_to_all.19 = bf16[8,16,712]{2,0,1:T(8,128)(2,1)S(1)} all-to-all(bf16[8,16,712]{2,0,1:T(8,128)(2,1)S(1)} %copy.6), channel_id=1, replica_groups=mesh['subj'=2,'row'=8,'col'=2] {'row','col'}, dimensions={1} | all-to-all | bytes 364544 | tf_op jit(solution)/shard_map/all_to_all | solution.py:59
  108.5 23.6 %all-gather.2.cloned.1.call-done = bf16[128,4096]{1,0:T(8,128)(2,1)} async-done(((bf16[8,4096]{1,0:T(8,128)(2,1)}), bf16[128,4096]{1,0:T(8,128)(2,1)}) %all-gather.2.cloned.1.call-update) | async-done | bytes 1048592 | tf_op jit(solution)/shard_map/all_gather | solution.py:61
  132.1 12.7 %multiply_convert_fusion = bf16[4096,712]{0,1:T(8,128)(2,1)} fusion(bf16[128,4096]{1,0:T(8,128)(2,1)} %all-gather.2.cloned.1.call-done, bf16[8,16,712]{2,0,1:T(8,128)(2,1)S(1)} %all_to_all.19), kind=kOutput, calls=%fused_computation | convolution fusion | flops 761167872 | bytes 7063552 | tf_op jit(solution)/shard_map/dot_general | solution.py:62
  (4 shorter events, 0.1 us)
Async XLA Ops:
  6.5 125.6 %all-gather.2.cloned.1.call-start = ((), (), s32[]{:S(2)}) async-start(), calls=%async_computation.1 | async-start | bytes 1114112 | tf_op jit(solution)/shard_map/all_gather | solution.py:61
  6.5 10.9 %collective-permute-start = (f32[8,11392]{1,0:T(8,128)}, f32[8,11392]{1,0:T(8,128)S(1)}, u32[]{:S(2)}, u32[]{:S(2)}) collective-permute-start(f32[8,11392]{1,0:T(8,128)} %param.5), channel_id=1, source_target_pairs={{0,1},{1,2},{2,3},{3,4},{4,5},{5,6},{6,7},{7,8},{8,9},{9,10},{10,1... | collective-permute-start | bytes 1093640 | tf_op jit(solution)/shard_map/ppermute | solution.py:19
  8.9 9.6 %collective-permute-start.1 = (f32[8,11392]{1,0:T(8,128)}, f32[8,11392]{1,0:T(8,128)S(1)}, u32[]{:S(2)}, u32[]{:S(2)}) collective-permute-start(f32[8,11392]{1,0:T(8,128)} %param.5), channel_id=1, source_target_pairs={{1,0},{2,1},{3,2},{4,3},{5,4},{6,5},{7,6},{8,7},{9,8},{10,9},{11,1... | collective-permute-start | bytes 1093640 | tf_op jit(solution)/shard_map/ppermute | solution.py:21
Sparse Core Ops, SparseCore 0:
  95.8 36.2 all-gather.1
where the time goes:
time: 152 us
  blocking collectives  76.2 us (50%)
  waiting for transfers between devices  23.6 us (16%)
  between operations  16.1 us (11%)
  other arithmetic  15.1 us (10%)
  matrix products  12.7 us (8%)
  local copies, waits for them, and re-layouts  4.28 us (3%)
  starting transfers between devices  3.66 us (2%)
    psum x1, blocking collectives, body(): spread = lax.psum(jnp.sum(centered * centered, axis=0), ('row', 'col'))  63.9 us
    all_gather x1, waiting for transfers between devices, body(): band_cols = lax.all_gather(band_slice, ('row', 'col'), axis=0, tiled=True)  23.6 us
    dot_general x1, matrix products, body(): lax.dot_general(band_cols, columns, (((0,), (0,)), ((), ())), preferred_e...  12.7 us
    reduce_sum x1, other arithmetic, body(): spread = lax.psum(jnp.sum(centered * centered, axis=0), ('row', 'col'))  12.4 us
    all_to_all x1, blocking collectives, body(): lax.all_to_all(scaled, ('row', 'col'), split_axis=1, concat_axis=0, tiled...  12.3 us
  transfers between devices with their start and end apart: 3, of which 1 were waited for; matrix products, arithmetic and copies ran while one was open for 4% of the time, Pallas kernels for 0%

commit v1 on v0

--- a/solution.py
+++ b/solution.py
@@ -54,7 +54,7 @@
     own_kept = kept_frames[lax.axis_index(("row", "col"))]
     keep_mask = (jnp.arange(block_len, dtype=jnp.int32) < own_kept).astype(jnp.float32)[:, None]
     centered = keep_mask * filtered
-    spread = lax.psum(jnp.sum(centered * centered, axis=0), ("row", "col"))
+    spread = lax.psum(lax.psum(jnp.sum(centered * centered, axis=0), "col"), "row")
     scaled = (centered * lax.rsqrt(spread + EPSILON)).astype(jnp.bfloat16)
     columns = lax.all_to_all(scaled, ("row", "col"), split_axis=1, concat_axis=0, tiled=True)
     band_slice = lax.dynamic_slice_in_dim(scaled, band_start[0], B, 1)

time: 152 us -> 133 us (0.88)
  blocking collectives: 76.2 us -> 57 us
    psum x1 -> x2, blocking collectives: 63.9 us -> 44.7 us  [the longest x1 38.1 us: body(): lax.psum(lax.psum(jnp.sum(centered * centered, axis=0), 'col'), 'row')]
where the time goes in v1:
time: 133 us; the launch traced here: 132 us
  blocking collectives  57 us (43%)
  waiting for transfers between devices  23.6 us (18%)
  between operations  16.1 us (12%)
  other arithmetic  15.1 us (11%)
  matrix products  12.7 us (10%)
  local copies, waits for them, and re-layouts  4.28 us (3%)
  starting transfers between devices  3.66 us (3%)
    psum x1, blocking collectives, body(): lax.psum(lax.psum(jnp.sum(centered * centered, axis=0), 'col'), 'row')  38.1 us
    all_gather x1, waiting for transfers between devices, body(): band_cols = lax.all_gather(band_slice, ('row', 'col'), axis=0, tiled=True)  23.6 us
    dot_general x1, matrix products, body(): lax.dot_general(band_cols, columns, (((0,), (0,)), ((), ())), preferred_e...  12.7 us
    reduce_sum x1, other arithmetic, body(): jnp.sum(centered * centered, axis=0)  12.4 us
    all_to_all x1, blocking collectives, body(): lax.all_to_all(scaled, ('row', 'col'), split_axis=1, concat_axis=0, tiled...  12.3 us
    psum x1, blocking collectives, body(): lax.psum(jnp.sum(centered * centered, axis=0), 'col')  6.59 us
  transfers between devices with their start and end apart: 3, of which 1 were waited for; matrix products, arithmetic and copies ran while one was open for 4% of the time, Pallas kernels for 0%

profile of v1, /device:TPU:0, one launch (start us, length us, event | category | flops | bytes accessed | tf_op | source)
XLA Modules:
  0.0 132.4 jit_solution(17430491446508163915)
XLA Ops:
  6.5 0.0 all-gather.2.cloned.1.call-start
  6.5 2.4 %collective-permute-start = (f32[8,11392]{1,0:T(8,128)}, f32[8,11392]{1,0:T(8,128)S(1)}, u32[]{:S(2)}, u32[]{:S(2)}) collective-permute-start(f32[8,11392]{1,0:T(8,128)} %param.5), channel_id=1, source_target_pairs={{0,1},{1,2},{2,3},{3,4},{4,5},{5,6},{6,7},{7,8},{8,9},{9,10},{10,1... | collective-permute-start | bytes 1093640 | tf_op jit(solution)/shard_map/ppermute | solution.py:19
  8.9 1.3 collective-permute-start.1
  10.9 1.3 dynamic_slice.6
  12.1 1.3 %convert_reduce_fusion = (f32[]{:T(128)}, f32[]{:T(128)}) fusion(s32[]{:T(128)} %bitcast.26, f32[17]{0:T(128)} %param.6), kind=kLoop, calls=%fused_computation.42 | loop fusion | flops 117 | bytes 80 | tf_op jit(solution)/shard_map/reduce_sum | solution.py:32
  13.5 0.6 compare_convert_fusion
  16.1 0.7 subtract_select_fusion
  16.7 0.7 fusion.19
  17.4 0.0 collective-permute-done
  17.5 1.0 constant_dynamic-update-slice_fusion
  18.5 0.0 collective-permute-done.1
  18.6 12.4 %multiply_reduce_fusion = (f32[11392]{0:T(1024)S(1)}, f32[8,11392]{1,0:T(8,128)S(1)}) fusion(f32[8,11392]{1,0:T(8,128)S(1)} %collective-permute-done.1, f32[]{:T(128)} %bitcast.18, f32[16,11392]{1,0:T(8,128)S(1)} %constant_dynamic-update-slice_fusion.2, f32[]{:T(128)} %bitcast.17, f32[]{:T(128)} %bitcast.16, f32[]{:T(128)} %bitcast.15, f32[]{:T(128)} %bitcast.14, ...), kind=kLoop, calls=%fused_computation.33 | loop fusion | flops 3269504 | bytes 6607460 | tf_op jit(solution)/shard_map/reduce_sum | solution.py:57
  31.0 6.6 %psum.14 = f32[11392]{0:T(1024)S(1)} all-reduce(f32[11392]{0:T(1024)S(1)} %get-tuple-element.5), channel_id=1, replica_groups=mesh['subj'=2,'row'=8,'col'=2] {'col'}, use_global_device_ids=true, to_apply=%region_3.0 | all-reduce | flops 11392 | bytes 91136 | tf_op jit(solution)/shard_map/psum | solution.py:57
  37.5 38.1 %psum.15 = f32[11392]{0:T(1024)S(1)} all-reduce(f32[11392]{0:T(1024)S(1)} %psum.14), channel_id=1, replica_groups=mesh['subj'=2,'row'=8,'col'=2] {'row'}, use_global_device_ids=true, to_apply=%region_4.0 | all-reduce | flops 11392 | bytes 91136 | tf_op jit(solution)/shard_map/psum | solution.py:57
  75.7 0.7 constant_dynamic-slice_fusion
  76.5 0.0 all-gather.2.cloned.1.call-update
  76.5 0.4 all_to_all.14
  76.9 0.1 copy.6
  77.0 12.3 %all_to_all.19 = bf16[8,16,712]{2,0,1:T(8,128)(2,1)S(1)} all-to-all(bf16[8,16,712]{2,0,1:T(8,128)(2,1)S(1)} %copy.6), channel_id=1, replica_groups=mesh['subj'=2,'row'=8,'col'=2] {'row','col'}, dimensions={1} | all-to-all | bytes 364544 | tf_op jit(solution)/shard_map/all_to_all | solution.py:59
  89.3 23.6 %all-gather.2.cloned.1.call-done = bf16[128,4096]{1,0:T(8,128)(2,1)} async-done(((bf16[8,4096]{1,0:T(8,128)(2,1)}), bf16[128,4096]{1,0:T(8,128)(2,1)}) %all-gather.2.cloned.1.call-update) | async-done | bytes 1048592 | tf_op jit(solution)/shard_map/all_gather | solution.py:61
  112.9 12.7 %multiply_convert_fusion = bf16[4096,712]{0,1:T(8,128)(2,1)} fusion(bf16[128,4096]{1,0:T(8,128)(2,1)} %all-gather.2.cloned.1.call-done, bf16[8,16,712]{2,0,1:T(8,128)(2,1)S(1)} %all_to_all.19), kind=kOutput, calls=%fused_computation | convolution fusion | flops 761167872 | bytes 7063552 | tf_op jit(solution)/shard_map/dot_general | solution.py:62
  (4 shorter events, 0.1 us)
Async XLA Ops:
  6.5 106.4 %all-gather.2.cloned.1.call-start = ((), (), s32[]{:S(2)}) async-start(), calls=%async_computation.1 | async-start | bytes 1114112 | tf_op jit(solution)/shard_map/all_gather | solution.py:61
  6.5 10.9 %collective-permute-start = (f32[8,11392]{1,0:T(8,128)}, f32[8,11392]{1,0:T(8,128)S(1)}, u32[]{:S(2)}, u32[]{:S(2)}) collective-permute-start(f32[8,11392]{1,0:T(8,128)} %param.5), channel_id=1, source_target_pairs={{0,1},{1,2},{2,3},{3,4},{4,5},{5,6},{6,7},{7,8},{8,9},{9,10},{10,1... | collective-permute-start | bytes 1093640 | tf_op jit(solution)/shard_map/ppermute | solution.py:19
  8.9 9.6 %collective-permute-start.1 = (f32[8,11392]{1,0:T(8,128)}, f32[8,11392]{1,0:T(8,128)S(1)}, u32[]{:S(2)}, u32[]{:S(2)}) collective-permute-start(f32[8,11392]{1,0:T(8,128)} %param.5), channel_id=1, source_target_pairs={{1,0},{2,1},{3,2},{4,3},{5,4},{6,5},{7,6},{8,7},{9,8},{10,9},{11,1... | collective-permute-start | bytes 1093640 | tf_op jit(solution)/shard_map/ppermute | solution.py:21
Sparse Core Ops, SparseCore 0:
  76.6 36.2 all-gather.1
